TPU v7x, 256 devices: a whole 4x4x8 slice. The times are simulated.
256 devices in a mesh: pair: 32 (over y, x, core), occ: 8 (over z).
Axes of the slice: x: 4, y: 4, z: 8, core: 2. Of those that a mesh axis runs over, the one named last changes fastest.
Arguments:
- half_ints: bfloat16 [8, 12288, 6144], P('occ', 'pair'), may hold values from -6 to 6
- pair_coef: bfloat16 [512, 12288], P('occ'), may hold values from -0.078125 to 0.078125
- mo_virtual: bfloat16 [5632, 6144], P('pair'), may hold values from -0.078125 to 0.078125
- screen: int32 [192], replicated, may hold values 0 or 1
- slot_block: int32 [192], replicated, may hold values from 0 to 191, each once
Outputs:
- mo_block: bfloat16 [5632, 8, 512], P('pair', 'occ')
Inputs may be any that keep to these rules, and one draw needn't show every extreme that they name: `screen`: 1 where the pair block survives screening, 0 where it is dropped. `slot_block`: each logical pair block stands in exactly one storage slot; index k of pair holds slots k * 6 to k * 6 + 5.
All inputs are finite; a program needn't handle non-finite values.
Results may differ from a plain program's by a relative error of at most 0.0049.
Values may be sent and summed in bfloat16 or wider, within the bound.
No kernel may reach another device: no remote copies, remote signals or barrier semaphores. Data moves between devices by JAX's collectives and lax.ppermute only.
A program may use at most 128 MiB of HBM per device.

v0:
```python
import jax
import jax.numpy as jnp
from jax import lax
from jax.sharding import PartitionSpec as P


def shards(half_ints, pair_coef, mo_virtual, screen, slot_block):
    coef_all = lax.all_gather(pair_coef, "occ", axis=0, tiled=True)
    occ_width = coef_all.shape[0]
    block_count = screen.shape[0]
    block_width = coef_all.shape[1] // block_count
    masked_coef = (
        coef_all.reshape(occ_width, block_count, block_width)
        * screen.astype(jnp.bfloat16)[None, :, None]
    )
    selected = jnp.take(masked_coef, slot_block, axis=1).reshape(
        occ_width, block_count * block_width
    )
    local_pairs = half_ints.shape[1]
    own_index = lax.axis_index("pair")
    local_cols = lax.dynamic_slice_in_dim(selected, own_index * local_pairs, local_pairs, 1)
    summed_pairs = lax.psum_scatter(
        jnp.einsum("jq,iqn->nij", local_cols, half_ints, preferred_element_type=jnp.float32),
        "pair",
        scatter_dimension=0,
        tiled=True,
    )
    occ_pair = summed_pairs.astype(jnp.bfloat16)
    item_width = occ_pair.shape[1] * occ_pair.shape[2]
    virt_count = mo_virtual.shape[0]
    block_part = lax.all_gather(occ_pair, "pair", axis=0, tiled=True)
    flat_rows = block_part.reshape(block_part.shape[0], item_width)
    folded = jnp.dot(mo_virtual, flat_rows, preferred_element_type=jnp.float32)
    return folded.reshape(virt_count, occ_pair.shape[1], occ_pair.shape[2]).astype(jnp.bfloat16)


def solution(mesh):
    placed = (P("occ", "pair", None), P("occ", None), P("pair", None), P(), P())
    return jax.shard_map(
        shards, mesh=mesh, in_specs=placed, out_specs=P("pair", "occ", None), check_vma=False
    )
```

profile of v0, /device:TPU:1, one launch (start us, length us, event | category | flops | bytes accessed | tf_op | source)
XLA Modules:
  0.0 1388.3 jit_solution(8234210186869820136)
XLA Ops:
  6.5 0.0 copy-start
  6.5 0.0 all-gather.3.cloned.1.call-start
  6.5 0.7 all-gather.3.cloned.1.call-update
  7.3 0.0 all-gather.5.cloned.1.call-start
  7.3 0.7 convert_element_type.15
  8.0 0.7 compare_and_fusion
  8.7 0.1 broadcast_in_dim.17
  8.8 0.1 broadcast_in_dim.18
  8.9 0.1 dynamic-slice.2
  9.0 1.3 dynamic-slice
  10.9 0.7 compare_select_fusion
  11.6 134.8 %all-gather.3.cloned.1.call-done = bf16[512,12288]{1,0:T(8,128)(2,1)} async-done(((bf16[64,12288]{1,0:T(8,128)(2,1)}), bf16[512,12288]{1,0:T(8,128)(2,1)}) %all-gather.3.cloned.1.call-update) | async-done | bytes 12582928 | tf_op jit(solution)/shard_map/all_gather | solution.py:8
  146.4 16.6 %copy.7 = bf16[512,12288]{0,1:T(8,128)(2,1)} copy(bf16[512,12288]{1,0:T(8,128)(2,1)} %all-gather.3.cloned.1.call-done) | data formatting | bytes 25165824 | tf_op jit(solution)/shard_map/all_gather | solution.py:8
  163.0 10.6 broadcast_multiply_fusion
  173.6 12.8 gather_fusion
  186.5 10.5 convolution_bitcast_fusion
  196.9 27.0 %copy.8 = f32[6144,1,512]{2,1,0:T(1,128)} copy(f32[6144,1,512]{0,2,1:T(8,128)} %convolution_bitcast_fusion) | data formatting | bytes 25165824 | tf_op jit(solution)/shard_map/jq,iqn->nij/transpose | solution.py:23
  224.0 1093.3 %all-reduce.2 = bf16[6144,1,512]{2,1,0:T(2,128)(2,1)} all-reduce(f32[6144,1,512]{2,1,0:T(1,128)} %copy.8), channel_id=2, replica_groups=mesh['pair'=32,'occ'=8] {'pair'}, use_global_device_ids=true, to_apply=%region_0.1.clone | all-reduce | flops 3145728 | bytes 18874368
  1317.3 1.4 dynamic-slice_convert_fusion
  1318.7 0.7 copy.9
  1319.4 0.0 all-gather.5.cloned.1.call-update
  1319.4 57.3 %all-gather.5.cloned.1.call-done = bf16[6144,1,512]{2,0,1:T(8,128)(2,1)} async-done(((bf16[192,1,512]{2,0,1:T(8,128)(2,1)}), bf16[6144,1,512]{2,0,1:T(8,128)(2,1)}) %all-gather.5.cloned.1.call-update) | async-done | bytes 6291472 | tf_op jit(solution)/shard_map/all_gather | solution.py:31
  1376.7 0.0 copy-done
  1376.7 4.7 fusion.6
  (1 shorter events, 0.0 us)
Async XLA Ops:
  6.5 1370.2 %copy-start = (bf16[176,6144]{1,0:T(8,128)(2,1)S(1)}, bf16[176,6144]{1,0:T(8,128)(2,1)}, u32[]{:S(2)}) copy-start(bf16[176,6144]{1,0:T(8,128)(2,1)} %param.7) | copy-start | bytes 6488068
  6.5 139.9 %all-gather.3.cloned.1.call-start = ((), (), s32[]{:S(2)}) async-start(), calls=%async_computation | async-start | bytes 14155776 | tf_op jit(solution)/shard_map/all_gather | solution.py:8
  7.3 1369.5 %all-gather.5.cloned.1.call-start = ((), (), s32[]{:S(2)}) async-start(), calls=%async_computation.1 | async-start | bytes 6488064 | tf_op jit(solution)/shard_map/all_gather | solution.py:31
Sparse Core Ops, SparseCore 0:
  9.1 137.2 all-gather.2
  1319.6 57.1 all-gather.4
where the time goes:
time: 1390 us
  blocking collectives  1090 us (78%)
  waiting for transfers between devices  193 us (14%)
  local copies, waits for them, and re-layouts  60.1 us (4%)
  matrix products  15.2 us (1%)
  between operations  14.1 us (1%)
    unnamed x1, blocking collectives  1090 us
    all_gather x1, waiting for transfers between devices, shards(): coef_all = lax.all_gather(pair_coef, 'occ', axis=0, tiled=True)  135 us
    all_gather x1, waiting for transfers between devices, shards(): block_part = lax.all_gather(occ_pair, 'pair', axis=0, tiled=True)  57.3 us
  transfers between devices with their start and end apart: 2, of which 2 were waited for; matrix products, arithmetic and copies ran while one was open for 0% of the time, Pallas kernels for 0%

commit v1 on v0

--- a/solution.py
+++ b/solution.py
@@ -5,7 +5,9 @@
 
 
 def shards(half_ints, pair_coef, mo_virtual, screen, slot_block):
-    coef_all = lax.all_gather(pair_coef, "occ", axis=0, tiled=True)
+    coef_all = jnp.concatenate(
+        lax.all_to_all(jnp.stack([pair_coef] * lax.axis_size("occ")), "occ", 0, 0), axis=0
+    )
     occ_width = coef_all.shape[0]
     block_count = screen.shape[0]
     block_width = coef_all.shape[1] // block_count

time: 1390 us -> 1590 us (1.14)
  waiting for transfers between devices: 193 us -> 331 us
  local copies, waits for them, and re-layouts: 60.1 us -> 112 us
    all_to_all x0 -> x1, waiting for transfers between devices: none -> 276 us  [shards(): lax.all_to_all(jnp.stack([pair_coef] * lax.axis_size('occ')), 'occ', 0, 0)]
    all_gather x1 -> x0, waiting for transfers between devices: 135 us -> none  [shards(): coef_all = lax.all_gather(pair_coef, 'occ', axis=0, tiled=True)]
    another operation x0 -> x3, local copies, waits for them, and re-layouts: none -> 68.9 us  [the longest x2 61.2 us: shards(): coef_all.reshape(occ_width, block_count, block_width)]
    all_gather x1 -> x0, local copies, waits for them, and re-layouts: 16.6 us -> none  [shards(): coef_all = lax.all_gather(pair_coef, 'occ', axis=0, tiled=True)]
where the time goes in v1:
time: 1590 us; the launch traced here: 1580 us
  blocking collectives  1090 us (69%)
  waiting for transfers between devices  331 us (21%)
  local copies, waits for them, and re-layouts  112 us (7%)
    unnamed x1, blocking collectives  1090 us
    all_to_all x1, waiting for transfers between devices, shards(): lax.all_to_all(jnp.stack([pair_coef] * lax.axis_size('occ')), 'occ', 0, 0)  276 us
    another operation x2, local copies, waits for them, and re-layouts, shards(): coef_all.reshape(occ_width, block_count, block_width)  61.2 us
    all_gather x1, waiting for transfers between devices, shards(): block_part = lax.all_gather(occ_pair, 'pair', axis=0, tiled=True)  55 us
  transfers between devices with their start and end apart: 2, of which 2 were waited for; matrix products, arithmetic and copies ran while one was open for 0% of the time, Pallas kernels for 0%

profile of v1, /device:TPU:1, one launch (start us, length us, event | category | flops | bytes accessed | tf_op | source)
XLA Modules:
  0.0 1584.8 jit_solution(17412149255229692608)
XLA Ops:
  6.5 0.0 copy-start
  6.5 7.7 stack.2
  14.3 0.0 copy-start.2
  14.3 0.0 copy-start.1
  14.3 0.0 copy-start.3
  14.3 9.1 all-to-all-start
  23.4 0.0 all-gather.2.cloned.1.call-start
  23.5 0.0 copy-done.2
  23.5 0.0 copy-done.1
  23.5 0.1 broadcast_in_dim.17
  23.6 0.1 broadcast_in_dim.18
  23.7 0.1 dynamic-slice.2
  23.8 0.0 copy-done.3
  23.8 0.6 dynamic-slice
  25.1 275.7 %all-to-all-done = bf16[8,64,12288]{2,1,0:T(8,128)(2,1)} async-done(((bf16[8,64,12288]{2,1,0:T(8,128)(2,1)}), bf16[8,64,12288]{2,1,0:T(8,128)(2,1)}, u32[]{:S(2)}, u32[]{:S(2)}) %all-to-all-start) | async-done | bytes 12582944 | tf_op jit(solution)/shard_map/all_to_all | solution.py:9
  300.7 34.4 %reshape_reshape.3 = bf16[512,192,64]{2,1,0:T(8,128)(2,1)} reshape(bf16[8,64,12288]{2,1,0:T(8,128)(2,1)} %all-to-all-done) | data formatting | bytes 25165824 | tf_op jit(solution)/shard_map/reshape;reshape | solution.py:15
  335.1 26.8 %copy.7 = bf16[512,192,64]{0,2,1:T(8,128)(2,1)} copy(bf16[512,192,64]{2,1,0:T(8,128)(2,1)} %reshape_reshape.3) | data formatting | bytes 25165824 | tf_op jit(solution)/shard_map/reshape;reshape | solution.py:15
  361.9 10.7 broadcast_multiply_fusion
  372.6 12.8 gather_fusion
  385.4 10.5 convolution_bitcast_fusion
  395.9 27.0 %copy.8 = f32[6144,1,512]{2,1,0:T(1,128)} copy(f32[6144,1,512]{0,2,1:T(8,128)} %convolution_bitcast_fusion) | data formatting | bytes 25165824 | tf_op jit(solution)/shard_map/jq,iqn->nij/transpose | solution.py:25
  422.9 1093.1 %all-reduce.2 = bf16[6144,1,512]{2,1,0:T(2,128)(2,1)} all-reduce(f32[6144,1,512]{2,1,0:T(1,128)} %copy.8), channel_id=2, replica_groups=mesh['pair'=32,'occ'=8] {'pair'}, use_global_device_ids=true, to_apply=%region_0.1.clone | all-reduce | flops 3145728 | bytes 18874368
  1516.1 1.4 dynamic-slice_convert_fusion
  1517.5 0.7 copy.9
  1518.2 0.0 all-gather.2.cloned.1.call-update
  1518.2 55.0 %all-gather.2.cloned.1.call-done = bf16[6144,1,512]{2,0,1:T(8,128)(2,1)} async-done(((bf16[192,1,512]{2,0,1:T(8,128)(2,1)}), bf16[6144,1,512]{2,0,1:T(8,128)(2,1)}) %all-gather.2.cloned.1.call-update) | async-done | bytes 6291472 | tf_op jit(solution)/shard_map/all_gather | solution.py:33
  1573.2 0.0 copy-done
  1573.2 4.7 fusion.6
  (4 shorter events, 0.0 us)
Async XLA Ops:
  6.5 1566.7 %copy-start = (bf16[176,6144]{1,0:T(8,128)(2,1)S(1)}, bf16[176,6144]{1,0:T(8,128)(2,1)}, u32[]{:S(2)}) copy-start(bf16[176,6144]{1,0:T(8,128)(2,1)} %param.7) | copy-start | bytes 6488068
  14.3 9.2 copy-start.2
  14.3 9.2 copy-start.1
  14.3 9.5 copy-start.3
  14.3 286.5 %all-to-all-start = ((bf16[8,64,12288]{2,1,0:T(8,128)(2,1)}), bf16[8,64,12288]{2,1,0:T(8,128)(2,1)}, u32[]{:S(2)}, u32[]{:S(2)}) async-start(bf16[8,64,12288]{2,1,0:T(8,128)(2,1)} %stack.2), calls=%async_computation | async-start | bytes 25165824 | tf_op jit(solution)/shard_map/all_to_all | solution.py:9
  23.4 1549.8 %all-gather.2.cloned.1.call-start = ((), (), s32[]{:S(2)}) async-start(), calls=%async_computation.1 | async-start | bytes 6488064 | tf_op jit(solution)/shard_map/all_gather | solution.py:33
Sparse Core Ops, SparseCore 0:
  1518.3 54.8 all-gather.1
